TPU v7x, 128 devices: a whole 4x4x4 slice. The times are simulated.
128 devices in a mesh: wide: 16 (over x, y_hi, core), narrow: 8 (over z, y_lo).
Axes of the slice: x: 4, y: 4 (y_hi: 2, y_lo: 2; y = y_hi * 2 + y_lo), z: 4, core: 2. Of those that a mesh axis runs over, the one named last changes fastest.
Arguments:
- dosages: int32 [2048, 24576], P('narrow', 'wide'), may hold values from 0 to 3, as said below
- allele_counts: int32 [2048], P('narrow'), may hold values from 4000 to 384000, as said below
- called_counts: int32 [2048], P('narrow'), may hold values from 200000 to 400000
Outputs:
- relation: float32 [16, 8, 192, 24576], P(None, 'narrow', None, 'wide')
Inputs may be any that keep to these rules, and one draw needn't show every extreme that they name: 3 marks a missing call; 0, 1 and 2 are dosages. `allele_counts`: the floor of the SNP's called_counts times a whole number p from 1 to 48, divided by 50, so that freq lies in (0, 0.5).
All inputs are finite; a program needn't handle non-finite values.
Results may differ from a plain program's by a relative error of at most 0.0043.
Values may be sent and summed in bfloat16 or wider, within the bound.
A program may use at most 128 MiB of HBM per device.

v0:
```python
import jax
import jax.numpy as jnp
from jax import lax
from jax.sharding import PartitionSpec as P

SNPS = 2048


def standardize(dosages, allele_counts, called_counts):
    freq = allele_counts.astype(jnp.float32) / (2.0 * called_counts.astype(jnp.float32))
    freq = freq[:, None]
    values = (dosages.astype(jnp.float32) - 2.0 * freq) * lax.rsqrt(2.0 * freq * (1.0 - freq))
    values = jnp.where(dosages == 3, jnp.zeros_like(values), values)
    return values.astype(jnp.bfloat16)


def shards(dosages, allele_counts, called_counts):
    standard = standardize(dosages, allele_counts, called_counts)
    sub_width = standard.shape[1] // lax.axis_size("narrow")
    block_rows = lax.all_gather(standard, "narrow", axis=0, tiled=True)
    position = lax.axis_index("narrow") * sub_width
    panel = lax.dynamic_slice_in_dim(block_rows, position, sub_width, 1)
    col_count = block_rows.shape[1]
    gathered = lax.all_gather(panel, "wide", axis=1, tiled=True)
    result = (
        lax.dot_general(
            gathered, block_rows, (((0,), (0,)), ((), ())), preferred_element_type=jnp.float32
        )
        / SNPS
    )
    return result.reshape(lax.axis_size("wide"), 1, sub_width, col_count)


def solution(mesh):
    return jax.shard_map(
        shards,
        mesh=mesh,
        in_specs=(P("narrow", "wide"), P("narrow"), P("narrow")),
        out_specs=P(None, "narrow", None, "wide"),
        check_vma=False,
    )
```

profile of v0, /device:TPU:1, one launch (start us, length us, event | category | flops | bytes accessed | tf_op | source)
XLA Modules:
  0.0 269.7 jit_solution(2306122670743038809)
XLA Ops:
  6.5 0.0 all-gather.3.cloned.1.call-start
  6.5 0.7 broadcast_multiply_fusion
  7.2 1.9 copy.5
  9.1 1.2 select_convert_fusion
  10.3 0.0 all-gather.3.cloned.1.call-update
  10.3 0.0 all-gather.5.cloned.1.call-start
  10.4 131.8 %all-gather.3.cloned.1.call-done = bf16[2048,1536]{0,1:T(8,128)(2,1)} async-done(((bf16[256,1536]{0,1:T(8,128)(2,1)}), bf16[2048,1536]{0,1:T(8,128)(2,1)}) %all-gather.3.cloned.1.call-update) | async-done | bytes 6291472 | tf_op jit(solution)/shard_map/all_gather | solution.py:20
  142.2 2.1 constant_dynamic-slice_fusion
  144.3 0.0 all-gather.5.cloned.1.call-update
  144.4 92.3 %all-gather.5.cloned.1.call-done = bf16[2048,3072]{0,1:T(8,128)(2,1)} async-done(((bf16[2048,192]{0,1:T(8,128)(2,1)}), bf16[2048,3072]{0,1:T(8,128)(2,1)}) %all-gather.5.cloned.1.call-update) | async-done | bytes 12582928 | tf_op jit(solution)/shard_map/all_gather | solution.py:24
  236.6 26.2 %convolution_multiply_fusion = f32[3072,1536]{1,0:T(8,128)} fusion(bf16[2048,3072]{0,1:T(8,128)(2,1)} %all-gather.5.cloned.1.call-done, bf16[2048,1536]{0,1:T(8,128)(2,1)} %all-gather.3.cloned.1.call-done), kind=kOutput, calls=%fused_computation | convolution fusion | flops 19332071424 | bytes 37748736 | tf_op jit(solution)/shard_map/dot_general | solution.py:26
  (1 shorter events, 0.0 us)
Async XLA Ops:
  6.5 135.7 %all-gather.3.cloned.1.call-start = ((), (), s32[]{:S(2)}) async-start(), calls=%async_computation | async-start | bytes 7077888 | tf_op jit(solution)/shard_map/all_gather | solution.py:20
  10.3 226.3 %all-gather.5.cloned.1.call-start = ((), (), s32[]{:S(2)}) async-start(), calls=%async_computation.1 | async-start | bytes 13369344 | tf_op jit(solution)/shard_map/all_gather | solution.py:24
Sparse Core Ops, SparseCore 0:
  10.5 131.7 all-gather.2
  144.6 91.9 all-gather.4
where the time goes:
time: 270 us
  waiting for transfers between devices  224 us (83%)
  matrix products  26.2 us (10%)
  between operations  13.4 us (5%)
  local copies, waits for them, and re-layouts  3.97 us (1%)
    all_gather x1, waiting for transfers between devices, shards(): block_rows = lax.all_gather(standard, 'narrow', axis=0, tiled=True)  132 us
    all_gather x1, waiting for transfers between devices, shards(): gathered = lax.all_gather(panel, 'wide', axis=1, tiled=True)  92.3 us
    dot_general x1, matrix products, shards(): lax.dot_general(gathered, block_rows, (((0,), (0,)), ((), ())), preferred...  26.2 us
  transfers between devices with their start and end apart: 2, of which 2 were waited for; matrix products, arithmetic and copies ran while one was open for 0% of the time, Pallas kernels for 0%

commit v1 on v0

v1 whole, which is shorter than its diff:
```python
import functools

import jax
import jax.numpy as jnp
from jax import lax
from jax.experimental import pallas as pl
from jax.experimental.pallas import tpu as pltpu
from jax.sharding import PartitionSpec as P

MESH = pl.DeviceIdType.MESH
SNPS = 2048
SUB = 192
NARROW = 8
WIDE = 16
PIECE = SNPS // NARROW
CHUNK = 2 * PIECE
STEPS = (0, 1, 3, 2)
PEERS = ((0, 1), (1, 0), (3, 0), (1, 1), (3, 1), (2, 0), (2, 1))


def standardize(dosages, allele_counts, called_counts):
    freq = allele_counts.astype(jnp.float32) / (2.0 * called_counts.astype(jnp.float32))
    freq = freq[:, None]
    values = (dosages.astype(jnp.float32) - 2.0 * freq) * lax.rsqrt(2.0 * freq * (1.0 - freq))
    values = jnp.where(dosages == 3, jnp.zeros_like(values), values)
    return values.astype(jnp.bfloat16)


def gather_kernel(own_ref, wide_ref, narrow_ref, a2a_send, a2a_recv, local_sem, far_send, far_recv, sib_send, sib_recv, near_send, near_recv):
    w, n = lax.axis_index("wide"), lax.axis_index("narrow")
    x, yh, c = w // 4, (w // 2) % 2, w % 2
    z, yl = n // 2, n % 2

    def wide_id(dx, flip, core):
        return ((x + dx) % 4) * 4 + (1 - yh if flip else yh) * 2 + (1 - c if core else c)

    def narrow_id(dz, flip):
        return ((z + dz) % 4) * 2 + (1 - yl if flip else yl)

    def at_wide(dx, flip, core):
        return {"wide": wide_id(dx, flip, core), "narrow": n}

    def at_narrow(dz, flip):
        return {"wide": w, "narrow": narrow_id(dz, flip)}

    targets = [at_narrow(*p) for p in PEERS]
    targets += [at_wide(1, 0, 0), at_wide(3, 0, 0), at_wide(0, 1, 0), at_wide(0, 0, 1)]
    barrier = pltpu.get_barrier_semaphore()
    for t in targets:
        pl.semaphore_signal(barrier, inc=1, device_id=t, device_id_type=MESH)
    pl.semaphore_wait(barrier, len(targets))

    def lanes(start, size):
        return pl.ds(pl.multiple_of(start, size), size)

    def piece(ref, slot, k):
        return ref.at[slot, :, lanes(k * PIECE, PIECE)]

    def chunk(ref, slot, k):
        return ref.at[slot, :, lanes(k * CHUNK, CHUNK)]

    sent = []

    def send(src, dst, ssem, rsem, device):
        copy = pltpu.make_async_remote_copy(
            src_ref=src, dst_ref=dst, send_sem=ssem, recv_sem=rsem, device_id=device, device_id_type=MESH
        )
        copy.start()
        sent.append(copy)

    def arrive(ref, ssem, rsem, device):
        pltpu.make_async_remote_copy(
            src_ref=ref, dst_ref=ref, send_sem=ssem, recv_sem=rsem, device_id=device, device_id_type=MESH
        ).wait_recv()

    for i, (dz, flip) in enumerate(PEERS):
        send(own_ref.at[narrow_id(dz, flip)], piece(wide_ref, w, n), a2a_send.at[i], a2a_recv.at[i], at_narrow(dz, flip))
    own_copy = pltpu.make_async_copy(own_ref.at[n], piece(wide_ref, w, n), local_sem.at[4])
    own_copy.start()

    def wide_far(dx, flip, k, way, device):
        slot = wide_id(dx, flip, 0)
        ref = chunk(wide_ref, slot, (z + STEPS[k]) % 4)
        send(ref, ref, far_send.at[way, k], far_recv.at[way, k], device)

    def wide_sib(dx, flip, k, way):
        slot = wide_id(dx, flip, 0)
        ref = chunk(wide_ref, slot, (z + STEPS[k]) % 4)
        send(ref, ref, sib_send.at[way, k], sib_recv.at[way, k], at_wide(0, 0, 1))

    def wide_arrive(dx, flip, k, way):
        ref = chunk(wide_ref, wide_id(dx, flip, 0), (z + STEPS[k]) % 4)
        arrive(ref, far_send.at[way, k], far_recv.at[way, k], at_wide(0, 1, 0))

    def near_far(dz, flip, k, way, device):
        ref = chunk(narrow_ref, narrow_id(dz, flip), (z + dz + STEPS[k]) % 4)
        send(ref, ref, near_send.at[way, k], near_recv.at[way, k], device)

    def near_arrive(dz, flip, k, way):
        ref = chunk(narrow_ref, narrow_id(dz, flip), (z + dz + STEPS[k]) % 4)
        arrive(ref, near_send.at[way, k], near_recv.at[way, k], at_narrow(0, 1))

    xp, xm, yhp = at_wide(1, 0, 0), at_wide(3, 0, 0), at_wide(0, 1, 0)
    zp, zm, ylp = at_narrow(1, 0), at_narrow(3, 0), at_narrow(0, 1)
    local = []

    def own_chunk(k):
        d = STEPS[k]
        if k == 0:
            own_copy.wait()
        for i, (dz, flip) in enumerate(PEERS):
            if (4 - dz) % 4 == d:
                arrive(piece(wide_ref, w, narrow_id(d, flip)), a2a_send.at[i], a2a_recv.at[i], ylp)
        wide_far(0, 0, k, 0, xp)
        wide_far(0, 0, k, 1, xm)
        wide_far(0, 0, k, 2, yhp)
        src = chunk(wide_ref, w, (z + d) % 4)
        dst = chunk(narrow_ref, n, (z + d) % 4)
        send(src, dst, near_send.at[0, k], near_recv.at[0, k], zp)
        send(src, dst, near_send.at[1, k], near_recv.at[1, k], zm)
        send(src, dst, near_send.at[2, k], near_recv.at[2, k], ylp)
        wide_sib(0, 0, k, 0)
        copy = pltpu.make_async_copy(src, dst, local_sem.at[k])
        copy.start()
        local.append(copy)

    def neighbours(k):
        wide_arrive(3, 0, k, 0)
        if k < 2:
            wide_far(3, 0, k, 3, xp)
        wide_sib(3, 0, k, 1)
        near_arrive(3, 0, k, 0)
        if k < 2:
            near_far(3, 0, k, 3, zp)
        wide_arrive(1, 0, k, 1)
        if k >= 2:
            wide_far(1, 0, k, 3, xm)
        wide_sib(1, 0, k, 2)
        near_arrive(1, 0, k, 1)
        if k >= 2:
            near_far(1, 0, k, 3, zm)

    def partners(k):
        wide_arrive(0, 1, k, 2)
        wide_far(0, 1, k, 4, xp)
        wide_far(0, 1, k, 5, xm)
        wide_sib(0, 1, k, 3)
        near_arrive(0, 1, k, 2)
        near_far(0, 1, k, 4, zp)
        near_far(0, 1, k, 5, zm)

    def partner_neighbours(k):
        wide_arrive(3, 1, k, 4)
        if k < 2:
            wide_far(3, 1, k, 6, xp)
        wide_sib(3, 1, k, 4)
        near_arrive(3, 1, k, 4)
        if k < 2:
            near_far(3, 1, k, 6, zp)
        wide_arrive(1, 1, k, 5)
        if k >= 2:
            wide_far(1, 1, k, 6, xm)
        wide_sib(1, 1, k, 5)
        near_arrive(1, 1, k, 5)
        if k >= 2:
            near_far(1, 1, k, 6, zm)

    def opposite(k, flip):
        way = 6 if flip else 3
        wide_arrive(2, flip, k, way)
        wide_sib(2, flip, k, 6 + flip)
        near_arrive(2, flip, k, way)

    for k in range(4):
        own_chunk(k)
    neighbours(0)
    neighbours(1)
    partners(0)
    neighbours(2)
    partners(1)
    neighbours(3)
    opposite(0, 0)
    opposite(2, 0)
    partners(2)
    opposite(1, 0)
    opposite(3, 0)
    partners(3)
    for k in range(4):
        partner_neighbours(k)
    for k in (0, 2, 1, 3):
        opposite(k, 1)
    order = ((0, 0), (3, 0), (1, 0), (0, 1), (3, 1), (1, 1), (2, 0), (2, 1))
    for way, (dx, flip) in enumerate(order):
        for k in range(4):
            ref = chunk(wide_ref, wide_id(dx, flip, 1), (z + STEPS[k]) % 4)
            arrive(ref, sib_send.at[way, k], sib_recv.at[way, k], at_wide(0, 0, 1))
    for copy in local:
        copy.wait()
    for copy in sent:
        copy.wait_send()


def gather(own, space):
    dma = pltpu.SemaphoreType.DMA
    return pl.pallas_call(
        gather_kernel,
        out_shape=(
            jax.ShapeDtypeStruct((WIDE, SUB, SNPS), jnp.bfloat16),
            jax.ShapeDtypeStruct((NARROW, SUB, SNPS), jnp.bfloat16),
        ),
        in_specs=[pl.BlockSpec(memory_space=pltpu.VMEM)],
        out_specs=(pl.BlockSpec(memory_space=space), pl.BlockSpec(memory_space=space)),
        scratch_shapes=[
            dma((7,)), dma((7,)), dma((5,)),
            dma((7, 4)), dma((7, 4)), dma((8, 4)), dma((8, 4)), dma((7, 4)), dma((7, 4)),
        ],
        compiler_params=pltpu.CompilerParams(collective_id=0, has_side_effects=True, vmem_limit_bytes=48 * 1024 * 1024),
    )(own)


def shards(dosages, allele_counts, called_counts):
    standard = standardize(dosages, allele_counts, called_counts)
    own = standard.T.reshape(NARROW, SUB, PIECE)
    wide, narrow = gather(own, pl.ANY)
    rows, cols = wide.reshape(WIDE * SUB, SNPS), narrow.reshape(NARROW * SUB, SNPS)
    result = lax.dot_general(rows, cols, (((1,), (1,)), ((), ())), preferred_element_type=jnp.float32) / SNPS
    return result.reshape(WIDE, 1, SUB, NARROW * SUB)


def solution(mesh):
    return jax.shard_map(
        shards,
        mesh=mesh,
        in_specs=(P("narrow", "wide"), P("narrow"), P("narrow")),
        out_specs=P(None, "narrow", None, "wide"),
        check_vma=False,
    )
```

time: 270 us -> 101 us (0.37)
  waiting for transfers between devices: 224 us -> 0 us
  Pallas kernels: 0 us -> 71.6 us
  between operations: 13.4 us -> 0.02 us
  local copies, waits for them, and re-layouts: 3.97 us -> 0.27 us
    all_gather x2 -> x0, waiting for transfers between devices: 224 us -> none  [the longest x1 132 us: shards(): block_rows = lax.all_gather(standard, 'narrow', axis=0, tiled=True)]
    pallas_call x0 -> x1, Pallas kernels: none -> 71.6 us  [gather(): pl.pallas_call(gather_kernel, out_shape=(jax.ShapeDtypeStruct((WIDE, SUB,...]
  transfers between devices with their start and end apart: 2 -> 0, of which waited for: 2 -> 0; matrix products, arithmetic and copies ran while one was open for 0% -> 0% of each run, Pallas kernels for 0% -> 0%
where the time goes in v1:
time: 101 us
  Pallas kernels  71.6 us (71%)
  matrix products  26.2 us (26%)
  other arithmetic  2.93 us (3%)
    pallas_call x1, Pallas kernels, gather(): pl.pallas_call(gather_kernel, out_shape=(jax.ShapeDtypeStruct((WIDE, SUB,...  71.6 us
    dot_general x1, matrix products, shards(): lax.dot_general(rows, cols, (((1,), (1,)), ((), ())), preferred_element_t...  26.2 us
    transpose x1, other arithmetic, shards(): own = standard.T.reshape(NARROW, SUB, PIECE)  2.23 us

profile of v1, /device:TPU:1, one launch (start us, length us, event | category | flops | bytes accessed | tf_op | source)
XLA Modules:
  0.0 101.1 jit_solution(349006390864288611)
XLA Ops:
  0.0 0.7 broadcast_multiply_fusion
  0.7 2.2 %fusion = bf16[1536,256]{0,1:T(8,128)(2,1)S(1)} fusion(s32[256,1536]{1,0:T(8,128)} %param.3, f32[256]{0:T(256)S(1)} %multiply_rsqrt_fusion, f32[256]{0:T(256)S(1)} %get-tuple-element.9), kind=kLoop, calls=%fused_computation.2 | loop fusion | flops 2359296 | bytes 2361344 | tf_op jit(solution)/shard_map/transpose | solution.py:223
  2.9 0.3 copy.4
  3.2 71.6 %shard_map.37 = (bf16[16,192,2048]{2,1,0:T(8,128)(2,1)}, bf16[8,192,2048]{2,1,0:T(8,128)(2,1)}) custom-call(bf16[8,192,256]{2,1,0:T(8,128)(2,1)S(1)} %bitcast.10), custom_call_target="tpu_custom_call" | custom-call | tf_op jit(solution)/shard_map/pallas_call | solution.py:205
  74.8 26.2 %convolution_multiply_fusion = f32[3072,1536]{1,0:T(8,128)} fusion(bf16[3072,2048]{1,0:T(8,128)(2,1)} %bitcast.11, bf16[1536,2048]{1,0:T(8,128)(2,1)} %bitcast.12), kind=kOutput, calls=%fused_computation | convolution fusion | flops 19332071424 | bytes 37748736 | tf_op jit(solution)/shard_map/dot_general | solution.py:226
  (1 shorter events, 0.0 us)

commit v2 on v0

v2 whole, which is shorter than its diff:
```python
import jax
import jax.numpy as jnp
from jax import lax
from jax.experimental import pallas as pl
from jax.experimental.pallas import tpu as pltpu
from jax.sharding import PartitionSpec as P

MESH = pl.DeviceIdType.MESH
SNPS = 2048
SUB = 192
NARROW = 8
WIDE = 16
BLK = NARROW * SUB
PIECE = SNPS // NARROW
QUARTER = SNPS // 4
ROWS = 2 * SUB
COLS = 4 * SUB
NEAR, OPPOSITE, FAR = 2, 4, 6


def standardize(dosages, allele_counts, called_counts):
    freq = allele_counts.astype(jnp.float32) / (2.0 * called_counts.astype(jnp.float32))
    freq = freq[:, None]
    values = (dosages.astype(jnp.float32) - 2.0 * freq) * lax.rsqrt(2.0 * freq * (1.0 - freq))
    values = jnp.where(dosages == 3, jnp.zeros_like(values), values)
    return values.astype(jnp.bfloat16)


def quarter_start(z, yl, q):
    half = z // 2
    return (yl if q < 2 else 1 - yl) * (SNPS // 2) + (half if q % 2 == 0 else 1 - half) * QUARTER


def tile(wide_ref, narrow_ref, start, i, j):
    lanes = pl.ds(pl.multiple_of(start, QUARTER), QUARTER)
    rows = wide_ref[pl.ds(2 * i, 2), :, lanes].reshape(ROWS, QUARTER)
    cols = narrow_ref[pl.ds(4 * j, 4), :, lanes].reshape(COLS, QUARTER)
    return lax.dot_general(rows, cols, (((1,), (1,)), ((), ())), preferred_element_type=jnp.float32)


def spot(i, j):
    return pl.ds(pl.multiple_of(i * ROWS, ROWS), ROWS), pl.ds(pl.multiple_of(j * COLS, COLS), COLS)


def gather_kernel(
    own_ref, wide_ref, narrow_ref, sum_ref,
    a2a_send, a2a_recv, local_sem, far_send, far_recv, sib_send, sib_recv, near_send, near_recv,
):
    w, n = lax.axis_index("wide"), lax.axis_index("narrow")
    x, yh, c = w // 4, (w // 2) % 2, w % 2
    z, yl = n // 2, n % 2

    def wide_id(dx, flip, core):
        return ((x + dx) % 4) * 4 + (1 - yh if flip else yh) * 2 + (1 - c if core else c)

    def ring(a):
        return (z, z + 1 - 2 * (z % 2), (z + 2) % 4, 3 - z)[a]

    def side(b):
        return 1 - yl if b else yl

    def narrow_id(label):
        return 2 * ring(label // 2) + side(label % 2)

    def at_wide(dx, flip, core):
        return {"wide": wide_id(dx, flip, core), "narrow": n}

    def at_narrow(label):
        return {"wide": w, "narrow": narrow_id(label)}

    xp, xm, yhp, sib = at_wide(1, 0, 0), at_wide(3, 0, 0), at_wide(0, 1, 0), at_wide(0, 0, 1)
    targets = [at_narrow(label) for label in range(1, NARROW)] + [xp, xm, yhp, sib]
    barrier = pltpu.get_barrier_semaphore()
    for t in targets:
        pl.semaphore_signal(barrier, inc=1, device_id=t, device_id_type=MESH)
    pl.semaphore_wait(barrier, len(targets))

    def slice_lanes(label):
        start = side(label % 2) * (SNPS // 2) + ring(label // 2) * PIECE
        return pl.ds(pl.multiple_of(start, PIECE), PIECE)

    def quarter_lanes(q, half=None):
        start = quarter_start(z, yl, q)
        if half is None:
            return pl.ds(pl.multiple_of(start, QUARTER), QUARTER)
        return pl.ds(pl.multiple_of(start + half * PIECE, PIECE), PIECE)

    sent = []

    def send(src, dst, ssem, rsem, device, keep=True):
        copy = pltpu.make_async_remote_copy(
            src_ref=src, dst_ref=dst, send_sem=ssem, recv_sem=rsem, device_id=device, device_id_type=MESH
        )
        copy.start()
        if keep:
            sent.append(copy)

    def described(ref, ssem, rsem, device):
        return pltpu.make_async_remote_copy(
            src_ref=ref, dst_ref=ref, send_sem=ssem, recv_sem=rsem, device_id=device, device_id_type=MESH
        )

    for label in (NEAR, FAR, OPPOSITE, 1, NEAR + 1, FAR + 1, OPPOSITE + 1):
        send(
            own_ref.at[narrow_id(label)], wide_ref.at[w, :, slice_lanes(0)],
            a2a_send.at[label - 1], a2a_recv.at[label - 1], at_narrow(label),
        )
    own_piece = pltpu.make_async_copy(own_ref.at[n], wide_ref.at[w, :, slice_lanes(0)], local_sem.at[4])
    own_piece.start()
    own_slice = pltpu.make_async_copy(own_ref, narrow_ref.at[:, :, slice_lanes(0)], local_sem.at[5])
    own_slice.start()
    local = [own_slice]
    groups = []

    def near_send_group(source, receiver, labels, sem):
        for i in labels:
            piece = receiver ^ i
            k = narrow_id(piece)
            lanes = slice_lanes(source)
            if source == 0:
                src = own_ref.at[k]
            elif piece == 0:
                src = wide_ref.at[w, :, lanes]
            else:
                src = narrow_ref.at[k, :, lanes]
            send(src, narrow_ref.at[k, :, lanes], near_send.at[sem], near_recv.at[sem], at_narrow(receiver), keep=False)
        groups.append((len(labels), source, sem, receiver))

    def near_arrive(count, source, sem):
        ref = narrow_ref.at[pl.ds(0, count), :, slice_lanes(source)]
        described(ref, near_send.at[sem], near_recv.at[sem], at_narrow(1)).wait_recv()

    def wide_send(dx, flip, q, sem, device, half=None):
        ref = wide_ref.at[wide_id(dx, flip, 0), :, quarter_lanes(q, half)]
        send(ref, ref, far_send.at[sem, q], far_recv.at[sem, q], device)

    def wide_arrive(dx, flip, q, sem, half=None):
        ref = wide_ref.at[wide_id(dx, flip, 0), :, quarter_lanes(q, half)]
        described(ref, far_send.at[sem, q], far_recv.at[sem, q], yhp).wait_recv()

    def share(dx, flip, q, sem):
        ref = wide_ref.at[wide_id(dx, flip, 0), :, quarter_lanes(q)]
        send(ref, ref, sib_send.at[sem, q], sib_recv.at[sem, q], sib)

    def own(q):
        labels = ((NEAR,), (FAR, OPPOSITE), (1, NEAR + 1), (FAR + 1, OPPOSITE + 1))[q]
        if q == 0:
            own_piece.wait()
        for label in labels:
            ref = wide_ref.at[w, :, slice_lanes(label)]
            described(ref, a2a_send.at[label - 1], a2a_recv.at[label - 1], at_narrow(1)).wait_recv()
        wide_send(0, 0, q, 0, xp)
        wide_send(0, 0, q, 1, xm)
        wide_send(0, 0, q, 2, yhp)
        share(0, 0, q, 0)
        lanes = slice_lanes(NEAR) if q == 0 else quarter_lanes(q)
        copy = pltpu.make_async_copy(wide_ref.at[w, :, lanes], narrow_ref.at[n, :, lanes], local_sem.at[q])
        copy.start()
        local.append(copy)

    def neighbours(q):
        wide_arrive(3, 0, q, 0)
        wide_send(3, 0, q, 5, xp, half=0)
        share(3, 0, q, 1)
        wide_arrive(1, 0, q, 1)
        wide_send(1, 0, q, 6, xm, half=1)
        share(1, 0, q, 2)

    def opposite(q):
        wide_arrive(2, 0, q, 5, half=0)
        wide_arrive(2, 0, q, 6, half=1)
        share(2, 0, q, 3)

    def partner(q):
        wide_arrive(0, 1, q, 2)
        wide_send(0, 1, q, 3, xp)
        wide_send(0, 1, q, 4, xm)
        share(0, 1, q, 4)

    def partner_neighbours(q):
        wide_arrive(3, 1, q, 3)
        wide_send(3, 1, q, 7, xp, half=0)
        share(3, 1, q, 5)
        wide_arrive(1, 1, q, 4)
        wide_send(1, 1, q, 8, xm, half=1)
        share(1, 1, q, 6)

    def partner_opposite(q):
        wide_arrive(2, 1, q, 7, half=0)
        wide_arrive(2, 1, q, 8, half=1)
        share(2, 1, q, 7)

    def shared(q):
        order = ((0, 0), (3, 0), (1, 0), (2, 0), (0, 1), (3, 1), (1, 1), (2, 1))
        for sem, (dx, flip) in enumerate(order):
            ref = wide_ref.at[wide_id(dx, flip, 1), :, quarter_lanes(q)]
            described(ref, sib_send.at[sem, q], sib_recv.at[sem, q], sib).wait_recv()

    def multiply(q, part):
        start = quarter_start(z, yl, q)

        def body(t, carry):
            i, j = 2 * part + t // 2, t % 2
            rows, cols = spot(i, j)
            value = tile(wide_ref, narrow_ref, start, i, j)
            if q:
                value = value + sum_ref[rows, cols]
            sum_ref[rows, cols] = value
            return carry

        lax.fori_loop(0, 4, body, 0)

    near_send_group(0, NEAR, (4, 5, 7), 0)
    near_send_group(0, FAR, (4, 5, 6, 7), 2)
    near_send_group(0, NEAR, (1, 2, 3, 6), 1)
    near_send_group(0, FAR, (1, 2, 3), 3)
    own(0)
    near_send_group(0, 1, (1, 2, 3, 4, 5, 6, 7), 4)
    own(1)
    neighbours(0)
    partner(0)
    own(2)
    near_arrive(4, FAR, 2)
    near_send_group(FAR, NEAR, (4 ^ NEAR, 5 ^ NEAR, 6 ^ NEAR, 7 ^ NEAR), 5)
    near_arrive(3, NEAR, 0)
    near_send_group(NEAR, FAR, (4 ^ FAR, 5 ^ FAR, 7 ^ FAR), 6)
    neighbours(1)
    opposite(0)
    partner_neighbours(0)
    own(3)
    partner_opposite(0)
    opposite(1)
    near_arrive(4, NEAR, 1)
    neighbours(2)
    shared(0)
    local[0].wait()
    local[1].wait()
    multiply(0, 0)
    multiply(0, 1)
    near_arrive(7, 1, 4)
    near_send_group(1, NEAR, (1, 4, 5, 7), 7)
    near_send_group(1, FAR, (4, 6, 7), 9)
    near_send_group(1, NEAR, (2, 3, 6), 8)
    near_send_group(1, FAR, (1, 2, 3, 5), 10)
    multiply(0, 2)
    multiply(0, 3)
    partner(1)
    neighbours(3)
    near_arrive(3, FAR, 3)
    near_arrive(4, OPPOSITE, 5)
    near_arrive(3, OPPOSITE, 6)
    partner_neighbours(1)
    partner(2)
    partner_opposite(1)
    shared(1)
    local[2].wait()
    multiply(1, 0)
    near_arrive(3, FAR + 1, 9)
    near_send_group(FAR + 1, NEAR, (4 ^ NEAR, 6 ^ NEAR, 7 ^ NEAR), 11)
    near_arrive(4, NEAR + 1, 7)
    near_send_group(NEAR + 1, FAR, (1 ^ FAR, 4 ^ FAR, 5 ^ FAR, 7 ^ FAR), 12)
    multiply(1, 1)
    partner(3)
    multiply(1, 2)
    partner_neighbours(2)
    multiply(1, 3)
    opposite(2)
    opposite(3)
    partner_opposite(2)
    near_arrive(3, NEAR + 1, 8)
    shared(2)
    local[3].wait()
    multiply(2, 0)
    partner_neighbours(3)
    multiply(2, 1)
    multiply(2, 2)
    multiply(2, 3)
    partner_opposite(3)
    near_arrive(4, FAR + 1, 10)
    near_arrive(3, OPPOSITE + 1, 11)
    near_arrive(4, OPPOSITE + 1, 12)
    shared(3)
    local[4].wait()
    for copy in sent:
        copy.wait_send()
    for count, source, sem, receiver in groups:
        ref = narrow_ref.at[pl.ds(0, count), :, slice_lanes(source)]
        described(ref, near_send.at[sem], near_recv.at[sem], at_narrow(receiver)).wait_send()


def finish_kernel(wide_ref, narrow_ref, sum_ref, out_ref, stage, sems):
    n = lax.axis_index("narrow")
    start = quarter_start(n // 2, n % 2, 3)

    def copy(i, slot):
        rows, _ = spot(i, 0)
        return pltpu.make_async_copy(stage.at[slot], out_ref.at[rows, :], sems.at[slot])

    def body(t, carry):
        for slot in range(2):
            i = 2 * t + slot

            @pl.when(t > 0)
            def _():
                copy(i - 2, slot).wait()

            for j in range(2):
                rows, cols = spot(i, j)
                value = tile(wide_ref, narrow_ref, start, i, j) + sum_ref[rows, cols]
                stage[slot, :, j * COLS:(j + 1) * COLS] = value * (1.0 / SNPS)
            copy(i, slot).start()
        return carry

    steps = WIDE // 4
    lax.fori_loop(0, steps, body, 0)
    for slot in range(2):
        copy(2 * steps - 2 + slot, slot).wait()


def product(own):
    dma = pltpu.SemaphoreType.DMA
    vmem = pl.BlockSpec(memory_space=pltpu.VMEM)
    wide, narrow, total = pl.pallas_call(
        gather_kernel,
        out_shape=(
            pltpu.VMEM((WIDE, SUB, SNPS), jnp.bfloat16),
            pltpu.VMEM((NARROW, SUB, SNPS), jnp.bfloat16),
            pltpu.VMEM((WIDE * SUB, BLK), jnp.float32),
        ),
        in_specs=[vmem],
        out_specs=(vmem, vmem, vmem),
        scratch_shapes=[
            dma((7,)), dma((7,)), dma((6,)),
            dma((9, 4)), dma((9, 4)), dma((8, 4)), dma((8, 4)), dma((13,)), dma((13,)),
        ],
        compiler_params=pltpu.CompilerParams(collective_id=0, has_side_effects=True, vmem_limit_bytes=12 * 1024 * 1024),
    )(own)
    return pl.pallas_call(
        finish_kernel,
        out_shape=jax.ShapeDtypeStruct((WIDE * SUB, BLK), jnp.float32),
        in_specs=[vmem, vmem, vmem],
        out_specs=pl.BlockSpec(memory_space=pl.ANY),
        scratch_shapes=[pltpu.VMEM((2, ROWS, BLK), jnp.float32), dma((2,))],
        compiler_params=pltpu.CompilerParams(vmem_limit_bytes=12 * 1024 * 1024),
    )(wide, narrow, total)


def shards(dosages, allele_counts, called_counts):
    standard = standardize(dosages, allele_counts, called_counts)
    own = standard.T.reshape(NARROW, SUB, PIECE)
    return product(own).reshape(WIDE, 1, SUB, BLK)


def solution(mesh):
    return jax.shard_map(
        shards,
        mesh=mesh,
        in_specs=(P("narrow", "wide"), P("narrow"), P("narrow")),
        out_specs=P(None, "narrow", None, "wide"),
        check_vma=False,
    )
```

time: 270 us -> 99.9 us (0.37)
  waiting for transfers between devices: 224 us -> 0 us
  Pallas kernels: 0 us -> 96.5 us
  matrix products: 26.2 us -> 0 us
  between operations: 13.4 us -> 0.02 us
  local copies, waits for them, and re-layouts: 3.97 us -> 0.27 us
    all_gather x2 -> x0, waiting for transfers between devices: 224 us -> none  [the longest x1 132 us: shards(): block_rows = lax.all_gather(standard, 'narrow', axis=0, tiled=True)]
    pallas_call x0 -> x2, Pallas kernels: none -> 96.5 us  [the longest x1 86.6 us: product(): pl.pallas_call(gather_kernel, out_shape=(pltpu.VMEM((WIDE, SUB, SNPS), jn...]
    dot_general x1 -> x0, matrix products: 26.2 us -> none  [shards(): lax.dot_general(gathered, block_rows, (((0,), (0,)), ((), ())), preferred...]
  transfers between devices with their start and end apart: 2 -> 0, of which waited for: 2 -> 0; matrix products, arithmetic and copies ran while one was open for 0% -> 0% of each run, Pallas kernels for 0% -> 0%
where the time goes in v2:
time: 99.9 us; the launch traced here: 99.8 us
  Pallas kernels  96.5 us (97%)
  other arithmetic  3.03 us (3%)
    pallas_call x1, Pallas kernels, product(): pl.pallas_call(gather_kernel, out_shape=(pltpu.VMEM((WIDE, SUB, SNPS), jn...  86.6 us
    pallas_call x1, Pallas kernels, product(): pl.pallas_call(finish_kernel, out_shape=jax.ShapeDtypeStruct((WIDE * SUB,...  9.83 us
    transpose x1, other arithmetic, shards(): own = standard.T.reshape(NARROW, SUB, PIECE)  2.32 us

profile of v2, /device:TPU:1, one launch (start us, length us, event | category | flops | bytes accessed | tf_op | source)
XLA Modules:
  0.0 99.8 jit_solution(10973824568559360865)
XLA Ops:
  0.0 0.7 broadcast_multiply_fusion
  0.7 2.3 %fusion = bf16[1536,256]{0,1:T(8,128)(2,1)S(1)} fusion(s32[256,1536]{1,0:T(8,128)} %param.3, f32[256]{0:T(256)S(1)} %multiply_rsqrt_fusion, f32[256]{0:T(256)S(1)} %get-tuple-element.11), kind=kLoop, calls=%fused_computation.1 | loop fusion | flops 2359296 | bytes 2361344 | tf_op jit(solution)/shard_map/transpose | solution.py:350
  3.0 0.3 copy.4
  3.3 86.6 %shard_map.37 = (bf16[16,192,2048]{2,1,0:T(8,128)(2,1)S(1)}, bf16[8,192,2048]{2,1,0:T(8,128)(2,1)S(1)}, f32[3072,1536]{1,0:T(8,128)S(1)}) custom-call(bf16[8,192,256]{2,1,0:T(8,128)(2,1)S(1)} %bitcast.6), custom_call_target="tpu_custom_call" | custom-call | tf_op jit(solution)/shard_map/pallas_call | solution.py:323
  90.0 9.8 %shard_map.38 = f32[3072,1536]{1,0:T(8,128)} custom-call(bf16[16,192,2048]{2,1,0:T(8,128)(2,1)S(1)} %get-tuple-element.8.wide_ref, bf16[8,192,2048]{2,1,0:T(8,128)(2,1)S(1)} %get-tuple-element.9.narrow_ref, f32[3072,1536]{1,0:T(8,128)S(1)} %get-tuple-element.10.sum_ref), custom_call_target="tpu_custom_call" | custom-call | tf_op jit(solution)/shard_map/pallas_call | solution.py:338
  (1 shorter events, 0.0 us)

commit v3 on v2

v3 whole, which is shorter than its diff:
```python
import jax
import jax.numpy as jnp
from jax import lax
from jax.experimental import pallas as pl
from jax.experimental.pallas import tpu as pltpu
from jax.sharding import PartitionSpec as P

MESH = pl.DeviceIdType.MESH
SNPS = 2048
SUB = 192
NARROW = 8
WIDE = 16
BLK = NARROW * SUB
PIECE = SNPS // NARROW
QUARTER = SNPS // 4
PARTS = 4
SLOTS = 4
ROWS = WIDE // PARTS * SUB
NEAR, OPPOSITE, FAR = 2, 4, 6


def standardize(dosages, allele_counts, called_counts):
    freq = allele_counts.astype(jnp.float32) / (2.0 * called_counts.astype(jnp.float32))
    freq = freq[:, None]
    values = (dosages.astype(jnp.float32) - 2.0 * freq) * lax.rsqrt(2.0 * freq * (1.0 - freq))
    values = jnp.where(dosages == 3, jnp.zeros_like(values), values)
    return values.astype(jnp.bfloat16)


def quarter_start(z, yl, q):
    half = z // 2
    return (yl if q < 2 else 1 - yl) * (SNPS // 2) + (half if q % 2 == 0 else 1 - half) * QUARTER


def tile(wide_ref, narrow_ref, start, panels):
    lanes = pl.ds(pl.multiple_of(start, QUARTER), QUARTER)
    rows = wide_ref[panels, :, lanes]
    rows = rows.reshape(rows.shape[0] * SUB, QUARTER)
    cols = narrow_ref[:, :, lanes].reshape(BLK, QUARTER)
    return lax.dot_general(rows, cols, (((1,), (1,)), ((), ())), preferred_element_type=jnp.float32)


def gather_kernel(
    own_ref, wide_ref, narrow_ref, sum_ref,
    a2a_send, a2a_recv, local_sem, far_send, far_recv, sib_send, sib_recv, near_send, near_recv,
):
    w, n = lax.axis_index("wide"), lax.axis_index("narrow")
    x, yh, c = w // 4, (w // 2) % 2, w % 2
    z, yl = n // 2, n % 2

    def wide_id(dx, flip, core):
        return ((x + dx) % 4) * 4 + (1 - yh if flip else yh) * 2 + (1 - c if core else c)

    def ring(a):
        return (z, z + 1 - 2 * (z % 2), (z + 2) % 4, 3 - z)[a]

    def side(b):
        return 1 - yl if b else yl

    def narrow_id(label):
        return 2 * ring(label // 2) + side(label % 2)

    def at_wide(dx, flip, core):
        return {"wide": wide_id(dx, flip, core), "narrow": n}

    def at_narrow(label):
        return {"wide": w, "narrow": narrow_id(label)}

    xp, xm, yhp, sib = at_wide(1, 0, 0), at_wide(3, 0, 0), at_wide(0, 1, 0), at_wide(0, 0, 1)
    targets = [at_narrow(label) for label in range(1, NARROW)] + [xp, xm, yhp, sib]
    barrier = pltpu.get_barrier_semaphore()
    for t in targets:
        pl.semaphore_signal(barrier, inc=1, device_id=t, device_id_type=MESH)
    pl.semaphore_wait(barrier, len(targets))

    def slice_lanes(label):
        start = side(label % 2) * (SNPS // 2) + ring(label // 2) * PIECE
        return pl.ds(pl.multiple_of(start, PIECE), PIECE)

    def quarter_lanes(q, half=None):
        if q == 0 and half is not None:
            return slice_lanes(NEAR if half else 0)
        start = quarter_start(z, yl, q)
        if half is None:
            return pl.ds(pl.multiple_of(start, QUARTER), QUARTER)
        return pl.ds(pl.multiple_of(start + half * PIECE, PIECE), PIECE)

    sent = []

    def send(src, dst, ssem, rsem, device, keep=True):
        copy = pltpu.make_async_remote_copy(
            src_ref=src, dst_ref=dst, send_sem=ssem, recv_sem=rsem, device_id=device, device_id_type=MESH
        )
        copy.start()
        if keep:
            sent.append(copy)

    def described(ref, ssem, rsem, device):
        return pltpu.make_async_remote_copy(
            src_ref=ref, dst_ref=ref, send_sem=ssem, recv_sem=rsem, device_id=device, device_id_type=MESH
        )

    def a2a(label):
        send(
            own_ref.at[narrow_id(label)], wide_ref.at[w, :, slice_lanes(0)],
            a2a_send.at[label - 1], a2a_recv.at[label - 1], at_narrow(label),
        )

    own_piece = pltpu.make_async_copy(own_ref.at[n], wide_ref.at[w, :, slice_lanes(0)], local_sem.at[4])
    own_piece.start()
    own_slice = pltpu.make_async_copy(own_ref, narrow_ref.at[:, :, slice_lanes(0)], local_sem.at[5])
    own_slice.start()
    local = [own_slice, own_piece]
    groups = {}

    def near_send_group(source, receiver, labels, sem):
        for i in labels:
            piece = receiver ^ i
            k = narrow_id(piece)
            lanes = slice_lanes(source)
            if source == 0:
                src = own_ref.at[k]
            elif piece == 0:
                src = wide_ref.at[w, :, lanes]
            else:
                src = narrow_ref.at[k, :, lanes]
            send(src, narrow_ref.at[k, :, lanes], near_send.at[sem], near_recv.at[sem], at_narrow(receiver), keep=False)
        groups[sem] = (groups.get(sem, (0,))[0] + len(labels), source, receiver)

    def near_arrive(count, source, sem):
        ref = narrow_ref.at[pl.ds(0, count), :, slice_lanes(source)]
        described(ref, near_send.at[sem], near_recv.at[sem], at_narrow(1)).wait_recv()

    def wide_send(dx, flip, q, sem, device, half=None):
        ref = wide_ref.at[wide_id(dx, flip, 0), :, quarter_lanes(q, half)]
        send(ref, ref, far_send.at[sem, q], far_recv.at[sem, q], device)

    def wide_arrive(dx, flip, q, sem, half=None):
        ref = wide_ref.at[wide_id(dx, flip, 0), :, quarter_lanes(q, half)]
        described(ref, far_send.at[sem, q], far_recv.at[sem, q], yhp).wait_recv()

    def share(dx, flip, q, sem, half=None):
        ref = wide_ref.at[wide_id(dx, flip, 0), :, quarter_lanes(q, half)]
        send(ref, ref, sib_send.at[sem, q], sib_recv.at[sem, q], sib)

    def first_half():
        src, dst = own_ref.at[n], wide_ref.at[w, :, quarter_lanes(0, 0)]
        for sem, device in ((9, xp), (10, xm), (11, yhp)):
            send(src, dst, far_send.at[sem, 0], far_recv.at[sem, 0], device)
        send(src, dst, sib_send.at[8, 0], sib_recv.at[8, 0], sib)

    def own(q):
        labels = ((NEAR,), (FAR, OPPOSITE), (1, NEAR + 1), (FAR + 1, OPPOSITE + 1))[q]
        for label in labels:
            ref = wide_ref.at[w, :, slice_lanes(label)]
            described(ref, a2a_send.at[label - 1], a2a_recv.at[label - 1], at_narrow(1)).wait_recv()
        half = None if q else 1
        wide_send(0, 0, q, 0, xp, half)
        wide_send(0, 0, q, 1, xm, half)
        if q == 0:
            to_partner(0)
        share(0, 0, q, 0, half)
        lanes = quarter_lanes(q, half)
        copy = pltpu.make_async_copy(wide_ref.at[w, :, lanes], narrow_ref.at[n, :, lanes], local_sem.at[q])
        copy.start()
        local.append(copy)

    def to_partner(q):
        wide_send(0, 0, q, 2, yhp, None if q else 1)

    def neighbours(q):
        if q == 0:
            wide_arrive(3, 0, 0, 9, half=0)
            wide_send(3, 0, 0, 5, xp, half=0)
            wide_arrive(1, 0, 0, 10, half=0)
            wide_arrive(1, 0, 0, 1, half=1)
            wide_send(1, 0, 0, 6, xm, half=1)
            wide_arrive(3, 0, 0, 0, half=1)
        else:
            wide_arrive(3, 0, q, 0)
            wide_send(3, 0, q, 5, xp, half=0)
            wide_arrive(1, 0, q, 1)
            wide_send(1, 0, q, 6, xm, half=1)
        share(3, 0, q, 1)
        share(1, 0, q, 2)

    def opposite(q):
        wide_arrive(2, 0, q, 5, half=0)
        wide_arrive(2, 0, q, 6, half=1)
        share(2, 0, q, 3)

    def partner(q):
        if q == 0:
            wide_arrive(0, 1, 0, 11, half=0)
        wide_arrive(0, 1, q, 2, None if q else 1)
        wide_send(0, 1, q, 3, xp, half=0)
        wide_send(0, 1, q, 4, xm, half=1)
        wide_send(0, 1, q, 12, xp, half=1)
        wide_send(0, 1, q, 13, xm, half=0)
        share(0, 1, q, 4)

    def partner_neighbours(q):
        wide_arrive(3, 1, q, 3, half=0)
        wide_send(3, 1, q, 7, xp, half=0)
        wide_arrive(1, 1, q, 4, half=1)
        wide_send(1, 1, q, 8, xm, half=1)

    def partner_opposite(q):
        wide_arrive(3, 1, q, 12, half=1)
        share(3, 1, q, 5)
        wide_arrive(1, 1, q, 13, half=0)
        share(1, 1, q, 6)
        wide_arrive(2, 1, q, 7, half=0)
        wide_arrive(2, 1, q, 8, half=1)
        share(2, 1, q, 7)

    def shared(q):
        order = ((0, 0), (3, 0), (1, 0), (2, 0), (0, 1), (3, 1), (1, 1), (2, 1))
        for sem, (dx, flip) in enumerate(order + ((0, 0),) * (q == 0)):
            half = {0: 1, 8: 0}.get(sem) if q == 0 else None
            ref = wide_ref.at[wide_id(dx, flip, 1), :, quarter_lanes(q, half)]
            described(ref, sib_send.at[sem, q], sib_recv.at[sem, q], sib).wait_recv()

    def multiply(q, part):
        start = quarter_start(z, yl, q)

        def body(p, carry):
            rows = pl.ds(pl.multiple_of(p * ROWS, ROWS), ROWS)
            value = tile(wide_ref, narrow_ref, start, pl.ds(p * (WIDE // PARTS), WIDE // PARTS))
            if q:
                value = value + sum_ref[rows, :]
            sum_ref[rows, :] = value
            return carry

        first = part + n // NARROW
        lax.fori_loop(first, first + 1, body, 0)

    a2a(NEAR)
    a2a(FAR)
    a2a(OPPOSITE)
    a2a(1)
    first_half()
    near_send_group(0, NEAR, (4, 5, 7), 0)
    near_send_group(0, FAR, (4, 5, 6, 7), 2)
    own(0)
    a2a(NEAR + 1)
    a2a(FAR + 1)
    a2a(OPPOSITE + 1)
    near_send_group(0, NEAR, (1, 2, 3, 6), 1)
    near_send_group(0, FAR, (1, 2, 3), 3)
    own(1)
    to_partner(1)
    neighbours(0)
    partner(0)
    near_send_group(0, 1, (4, 5, 6, 7), 4)
    near_send_group(0, 1, (1, 2, 3), 13)
    neighbours(1)
    opposite(0)
    partner_neighbours(0)
    own(2)
    near_arrive(4, FAR, 2)
    near_send_group(FAR, NEAR, (4 ^ NEAR, 5 ^ NEAR, 6 ^ NEAR, 7 ^ NEAR), 5)
    near_arrive(3, NEAR, 0)
    near_send_group(NEAR, FAR, (4 ^ FAR, 5 ^ FAR, 7 ^ FAR), 6)
    partner(1)
    near_arrive(4, 1, 4)
    near_send_group(1, NEAR, (4, 5, 7), 7)
    near_send_group(1, FAR, (1, 2, 3), 10)
    near_send_group(1, NEAR, (2, 6), 8)
    to_partner(2)
    partner_opposite(0)
    near_arrive(4, NEAR, 1)
    shared(0)
    local[0].wait()
    local[1].wait()
    local[2].wait()
    multiply(0, 0)
    multiply(0, 1)
    multiply(0, 2)
    neighbours(2)
    multiply(0, 3)
    partner_neighbours(1)
    own(3)
    to_partner(3)
    near_arrive(3, 1, 13)
    near_send_group(1, NEAR, (1,), 7)
    near_send_group(1, FAR, (4, 6, 7), 9)
    near_send_group(1, NEAR, (3,), 8)
    near_send_group(1, FAR, (5,), 10)
    opposite(1)
    partner(2)
    partner_opposite(1)
    near_arrive(3, FAR, 3)
    near_arrive(4, OPPOSITE, 5)
    near_arrive(3, OPPOSITE, 6)
    shared(1)
    local[3].wait()
    multiply(1, 0)
    multiply(1, 1)
    multiply(1, 2)
    neighbours(3)
    multiply(1, 3)
    partner_neighbours(2)
    partner(3)
    near_arrive(3, FAR + 1, 9)
    near_send_group(FAR + 1, NEAR, (4 ^ NEAR, 6 ^ NEAR, 7 ^ NEAR), 11)
    near_arrive(4, NEAR + 1, 7)
    near_send_group(NEAR + 1, FAR, (1 ^ FAR, 4 ^ FAR, 5 ^ FAR, 7 ^ FAR), 12)
    opposite(2)
    opposite(3)
    partner_opposite(2)
    near_arrive(3, NEAR + 1, 8)
    shared(2)
    local[4].wait()
    multiply(2, 0)
    partner_neighbours(3)
    multiply(2, 1)
    multiply(2, 2)
    multiply(2, 3)
    partner_opposite(3)
    near_arrive(4, FAR + 1, 10)
    near_arrive(3, OPPOSITE + 1, 11)
    near_arrive(4, OPPOSITE + 1, 12)
    shared(3)
    local[5].wait()
    for copy in sent:
        copy.wait_send()
    for sem, (count, source, receiver) in groups.items():
        ref = narrow_ref.at[pl.ds(0, count), :, slice_lanes(source)]
        described(ref, near_send.at[sem], near_recv.at[sem], at_narrow(receiver)).wait_send()


def finish_kernel(wide_ref, narrow_ref, sum_ref, out_ref, stage, sems):
    n = lax.axis_index("narrow")
    start = quarter_start(n // 2, n % 2, 3)
    copies = []
    panel = 0
    for i, count in enumerate((1, 1, 2, 2, 2, 2, 2, 2, 2)):
        slot, rows = i % SLOTS, slice(panel * SUB, (panel + count) * SUB)
        if i >= SLOTS:
            copies[i - SLOTS].wait()
        value = tile(wide_ref, narrow_ref, start, pl.ds(panel, count)) + sum_ref[rows, :]
        stage[slot, : count * SUB, :] = value * (1.0 / SNPS)
        copy = pltpu.make_async_copy(stage.at[slot, : count * SUB, :], out_ref.at[rows, :], sems.at[slot])
        copy.start()
        copies.append(copy)
        panel += count
    for copy in copies[-SLOTS:]:
        copy.wait()


def product(own):
    dma = pltpu.SemaphoreType.DMA
    vmem = pl.BlockSpec(memory_space=pltpu.VMEM)
    wide, narrow, total = pl.pallas_call(
        gather_kernel,
        out_shape=(
            pltpu.VMEM((WIDE, SUB, SNPS), jnp.bfloat16),
            pltpu.VMEM((NARROW, SUB, SNPS), jnp.bfloat16),
            pltpu.VMEM((WIDE * SUB, BLK), jnp.float32),
        ),
        in_specs=[vmem],
        out_specs=(vmem, vmem, vmem),
        scratch_shapes=[
            dma((7,)), dma((7,)), dma((6,)),
            dma((14, 4)), dma((14, 4)), dma((9, 4)), dma((9, 4)), dma((14,)), dma((14,)),
        ],
        compiler_params=pltpu.CompilerParams(collective_id=0, has_side_effects=True, vmem_limit_bytes=10 * 1024 * 1024),
    )(own)
    return pl.pallas_call(
        finish_kernel,
        out_shape=jax.ShapeDtypeStruct((WIDE * SUB, BLK), jnp.float32),
        in_specs=[vmem, vmem, vmem],
        out_specs=pl.BlockSpec(memory_space=pl.ANY),
        scratch_shapes=[pltpu.VMEM((SLOTS, 2 * SUB, BLK), jnp.float32), dma((SLOTS,))],
        compiler_params=pltpu.CompilerParams(vmem_limit_bytes=14 * 1024 * 1024),
    )(wide, narrow, total)


def shards(dosages, allele_counts, called_counts):
    standard = standardize(dosages, allele_counts, called_counts)
    own = standard.T.reshape(NARROW, SUB, PIECE)
    return product(own).reshape(WIDE, 1, SUB, BLK)


def solution(mesh):
    return jax.shard_map(
        shards,
        mesh=mesh,
        in_specs=(P("narrow", "wide"), P("narrow"), P("narrow")),
        out_specs=P(None, "narrow", None, "wide"),
        check_vma=False,
    )
```

time: 99.9 us -> 82.6 us (0.83)
  Pallas kernels: 96.5 us -> 79 us
    pallas_call x1, Pallas kernels: 86.6 us -> 70.9 us  [product(): pl.pallas_call(gather_kernel, out_shape=(pltpu.VMEM((WIDE, SUB, SNPS), jn...]
    pallas_call x1, Pallas kernels: 9.83 us -> 8.11 us  [product(): pl.pallas_call(finish_kernel, out_shape=jax.ShapeDtypeStruct((WIDE * SUB,...]
where the time goes in v3:
time: 82.6 us; the launch traced here: 82.5 us
  Pallas kernels  79 us (96%)
  other arithmetic  3.03 us (4%)
    pallas_call x1, Pallas kernels, product(): pl.pallas_call(gather_kernel, out_shape=(pltpu.VMEM((WIDE, SUB, SNPS), jn...  70.9 us
    pallas_call x1, Pallas kernels, product(): pl.pallas_call(finish_kernel, out_shape=jax.ShapeDtypeStruct((WIDE * SUB,...  8.11 us
    transpose x1, other arithmetic, shards(): own = standard.T.reshape(NARROW, SUB, PIECE)  2.32 us

profile of v3, /device:TPU:1, one launch (start us, length us, event | category | flops | bytes accessed | tf_op | source)
XLA Modules:
  0.0 82.5 jit_solution(10797394888249340004)
XLA Ops:
  0.0 0.7 broadcast_multiply_fusion
  0.7 2.3 %fusion = bf16[1536,256]{0,1:T(8,128)(2,1)S(1)} fusion(s32[256,1536]{1,0:T(8,128)} %param.3, f32[256]{0:T(256)S(1)} %multiply_rsqrt_fusion, f32[256]{0:T(256)S(1)} %get-tuple-element.11), kind=kLoop, calls=%fused_computation.1 | loop fusion | flops 2359296 | bytes 2361344 | tf_op jit(solution)/shard_map/transpose | solution.py:382
  3.0 0.3 copy.4
  3.3 70.9 %shard_map.37 = (bf16[16,192,2048]{2,1,0:T(8,128)(2,1)S(1)}, bf16[8,192,2048]{2,1,0:T(8,128)(2,1)S(1)}, f32[3072,1536]{1,0:T(8,128)S(1)}) custom-call(bf16[8,192,256]{2,1,0:T(8,128)(2,1)S(1)} %bitcast.6), custom_call_target="tpu_custom_call" | custom-call | tf_op jit(solution)/shard_map/pallas_call | solution.py:355
  74.2 8.1 %shard_map.38 = f32[3072,1536]{1,0:T(8,128)} custom-call(bf16[16,192,2048]{2,1,0:T(8,128)(2,1)S(1)} %get-tuple-element.8.wide_ref, bf16[8,192,2048]{2,1,0:T(8,128)(2,1)S(1)} %get-tuple-element.9.narrow_ref, f32[3072,1536]{1,0:T(8,128)S(1)} %get-tuple-element.10.sum_ref), custom_call_target="tpu_custom_call" | custom-call | tf_op jit(solution)/shard_map/pallas_call | solution.py:370
  (1 shorter events, 0.0 us)

commit v4 on v3

--- a/solution.py
+++ b/solution.py
@@ -19,12 +19,48 @@
 NEAR, OPPOSITE, FAR = 2, 4, 6
 
 
+def standardize_kernel(dosages_ref, allele_hbm, called_hbm, out_ref, blocks, allele_ref, called_ref, sems):
+    width = 2 * SUB
+    counts = []
+    for k, (src, dst) in enumerate(((allele_hbm, allele_ref), (called_hbm, called_ref))):
+        copy = pltpu.make_async_copy(src, dst, sems.at[4 + k])
+        copy.start()
+        counts.append(copy)
+    copies = []
+    for k in range(BLK // width):
+        copy = pltpu.make_async_copy(dosages_ref.at[:, k * width:(k + 1) * width], blocks.at[k], sems.at[k])
+        copy.start()
+        copies.append(copy)
+    for copy in counts:
+        copy.wait()
+    freq = allele_ref[...].astype(jnp.float32) / (2.0 * called_ref[...].astype(jnp.float32))
+    scale = lax.rsqrt(2.0 * freq * (1.0 - freq))
+    for k, copy in enumerate(copies):
+        copy.wait()
+        dosages = blocks[k].astype(jnp.float32).T
+        values = jnp.where(dosages == 3.0, 0.0, (dosages - 2.0 * freq) * scale)
+        out_ref[2 * k:2 * k + 2] = values.astype(jnp.bfloat16).reshape(2, SUB, PIECE)
+
+
+def hbm(array):
+    return pltpu.with_memory_space_constraint(array, pltpu.HBM)
+
+
 def standardize(dosages, allele_counts, called_counts):
-    freq = allele_counts.astype(jnp.float32) / (2.0 * called_counts.astype(jnp.float32))
-    freq = freq[:, None]
-    values = (dosages.astype(jnp.float32) - 2.0 * freq) * lax.rsqrt(2.0 * freq * (1.0 - freq))
-    values = jnp.where(dosages == 3, jnp.zeros_like(values), values)
-    return values.astype(jnp.bfloat16)
+    vmem = pl.BlockSpec(memory_space=pltpu.VMEM)
+    return pl.pallas_call(
+        standardize_kernel,
+        out_shape=pltpu.VMEM((NARROW, SUB, PIECE), jnp.bfloat16),
+        in_specs=[pl.BlockSpec(memory_space=pltpu.HBM)] * 3,
+        out_specs=vmem,
+        scratch_shapes=[
+            pltpu.VMEM((4, PIECE, 2 * SUB), jnp.int32),
+            pltpu.VMEM((1, PIECE), jnp.int32),
+            pltpu.VMEM((1, PIECE), jnp.int32),
+            pltpu.SemaphoreType.DMA((6,)),
+        ],
+        compiler_params=pltpu.CompilerParams(vmem_limit_bytes=8 * 1024 * 1024),
+    )(hbm(dosages), hbm(allele_counts.reshape(1, PIECE)), hbm(called_counts.reshape(1, PIECE)))
 
 
 def quarter_start(z, yl, q):
@@ -42,7 +78,7 @@
 
 def gather_kernel(
     own_ref, wide_ref, narrow_ref, sum_ref,
-    a2a_send, a2a_recv, local_sem, far_send, far_recv, sib_send, sib_recv, near_send, near_recv,
+    a2a_recv, local_sem, far_send, far_recv, sib_send, sib_recv, near_send, near_recv,
 ):
     w, n = lax.axis_index("wide"), lax.axis_index("narrow")
     x, yh, c = w // 4, (w // 2) % 2, w % 2
@@ -85,15 +121,10 @@
             return pl.ds(pl.multiple_of(start, QUARTER), QUARTER)
         return pl.ds(pl.multiple_of(start + half * PIECE, PIECE), PIECE)
 
-    sent = []
-
-    def send(src, dst, ssem, rsem, device, keep=True):
-        copy = pltpu.make_async_remote_copy(
+    def send(src, dst, ssem, rsem, device):
+        pltpu.make_async_remote_copy(
             src_ref=src, dst_ref=dst, send_sem=ssem, recv_sem=rsem, device_id=device, device_id_type=MESH
-        )
-        copy.start()
-        if keep:
-            sent.append(copy)
+        ).start()
 
     def described(ref, ssem, rsem, device):
         return pltpu.make_async_remote_copy(
@@ -103,7 +134,7 @@
     def a2a(label):
         send(
             own_ref.at[narrow_id(label)], wide_ref.at[w, :, slice_lanes(0)],
-            a2a_send.at[label - 1], a2a_recv.at[label - 1], at_narrow(label),
+            near_send, a2a_recv.at[label - 1], at_narrow(label),
         )
 
     own_piece = pltpu.make_async_copy(own_ref.at[n], wide_ref.at[w, :, slice_lanes(0)], local_sem.at[4])
@@ -111,7 +142,6 @@
     own_slice = pltpu.make_async_copy(own_ref, narrow_ref.at[:, :, slice_lanes(0)], local_sem.at[5])
     own_slice.start()
     local = [own_slice, own_piece]
-    groups = {}
 
     def near_send_group(source, receiver, labels, sem):
         for i in labels:
@@ -124,46 +154,45 @@
                 src = wide_ref.at[w, :, lanes]
             else:
                 src = narrow_ref.at[k, :, lanes]
-            send(src, narrow_ref.at[k, :, lanes], near_send.at[sem], near_recv.at[sem], at_narrow(receiver), keep=False)
-        groups[sem] = (groups.get(sem, (0,))[0] + len(labels), source, receiver)
+            send(src, narrow_ref.at[k, :, lanes], near_send, near_recv.at[sem], at_narrow(receiver))
 
     def near_arrive(count, source, sem):
         ref = narrow_ref.at[pl.ds(0, count), :, slice_lanes(source)]
-        described(ref, near_send.at[sem], near_recv.at[sem], at_narrow(1)).wait_recv()
+        described(ref, near_send, near_recv.at[sem], at_narrow(1)).wait_recv()
 
     def wide_send(dx, flip, q, sem, device, half=None):
         ref = wide_ref.at[wide_id(dx, flip, 0), :, quarter_lanes(q, half)]
-        send(ref, ref, far_send.at[sem, q], far_recv.at[sem, q], device)
+        send(ref, ref, far_send, far_recv.at[sem, q], device)
 
     def wide_arrive(dx, flip, q, sem, half=None):
         ref = wide_ref.at[wide_id(dx, flip, 0), :, quarter_lanes(q, half)]
-        described(ref, far_send.at[sem, q], far_recv.at[sem, q], yhp).wait_recv()
-
-    def share(dx, flip, q, sem, half=None):
+        described(ref, far_send, far_recv.at[sem, q], yhp).wait_recv()
+
+    def share(dx, flip, q, half=None):
         ref = wide_ref.at[wide_id(dx, flip, 0), :, quarter_lanes(q, half)]
-        send(ref, ref, sib_send.at[sem, q], sib_recv.at[sem, q], sib)
+        send(ref, ref, sib_send, sib_recv.at[q], sib)
 
     def first_half():
         src, dst = own_ref.at[n], wide_ref.at[w, :, quarter_lanes(0, 0)]
         for sem, device in ((9, xp), (10, xm), (11, yhp)):
-            send(src, dst, far_send.at[sem, 0], far_recv.at[sem, 0], device)
-        send(src, dst, sib_send.at[8, 0], sib_recv.at[8, 0], sib)
-
-    def own(q):
+            send(src, dst, far_send, far_recv.at[sem, 0], device)
+        send(src, dst, sib_send, sib_recv.at[0], sib)
+
+    def ready(q):
         labels = ((NEAR,), (FAR, OPPOSITE), (1, NEAR + 1), (FAR + 1, OPPOSITE + 1))[q]
         for label in labels:
             ref = wide_ref.at[w, :, slice_lanes(label)]
-            described(ref, a2a_send.at[label - 1], a2a_recv.at[label - 1], at_narrow(1)).wait_recv()
+            described(ref, near_send, a2a_recv.at[label - 1], at_narrow(1)).wait_recv()
+        lanes = quarter_lanes(q, None if q else 1)
+        copy = pltpu.make_async_copy(wide_ref.at[w, :, lanes], narrow_ref.at[n, :, lanes], local_sem.at[q])
+        copy.start()
+        local.append(copy)
+
+    def own(q):
         half = None if q else 1
         wide_send(0, 0, q, 0, xp, half)
         wide_send(0, 0, q, 1, xm, half)
-        if q == 0:
-            to_partner(0)
-        share(0, 0, q, 0, half)
-        lanes = quarter_lanes(q, half)
-        copy = pltpu.make_async_copy(wide_ref.at[w, :, lanes], narrow_ref.at[n, :, lanes], local_sem.at[q])
-        copy.start()
-        local.append(copy)
+        share(0, 0, q, half)
 
     def to_partner(q):
         wide_send(0, 0, q, 2, yhp, None if q else 1)
@@ -181,25 +210,37 @@
             wide_send(3, 0, q, 5, xp, half=0)
             wide_arrive(1, 0, q, 1)
             wide_send(1, 0, q, 6, xm, half=1)
-        share(3, 0, q, 1)
-        share(1, 0, q, 2)
+        share(3, 0, q)
+        share(1, 0, q)
 
     def opposite(q):
         wide_arrive(2, 0, q, 5, half=0)
         wide_arrive(2, 0, q, 6, half=1)
-        share(2, 0, q, 3)
+        share(2, 0, q)
+
+    def opposite_to_partner(q):
+        wide_send(2, 0, q, 7, yhp)
+
+    def partner_first():
+        wide_arrive(0, 1, 0, 11, half=0)
+        wide_send(0, 1, 0, 3, xp, half=0)
+        wide_send(0, 1, 0, 13, xm, half=0)
 
     def partner(q):
-        if q == 0:
-            wide_arrive(0, 1, 0, 11, half=0)
         wide_arrive(0, 1, q, 2, None if q else 1)
-        wide_send(0, 1, q, 3, xp, half=0)
+        if q:
+            wide_send(0, 1, q, 3, xp, half=0)
         wide_send(0, 1, q, 4, xm, half=1)
         wide_send(0, 1, q, 12, xp, half=1)
-        wide_send(0, 1, q, 13, xm, half=0)
-        share(0, 1, q, 4)
+        if q:
+            wide_send(0, 1, q, 13, xm, half=0)
+        share(0, 1, q)
 
     def partner_neighbours(q):
+        if q == 2:
+            wide_arrive(3, 1, q, 3, half=0)
+            wide_arrive(1, 1, q, 4, half=1)
+            return
         wide_arrive(3, 1, q, 3, half=0)
         wide_send(3, 1, q, 7, xp, half=0)
         wide_arrive(1, 1, q, 4, half=1)
@@ -207,19 +248,19 @@
 
     def partner_opposite(q):
         wide_arrive(3, 1, q, 12, half=1)
-        share(3, 1, q, 5)
+        share(3, 1, q)
         wide_arrive(1, 1, q, 13, half=0)
-        share(1, 1, q, 6)
-        wide_arrive(2, 1, q, 7, half=0)
-        wide_arrive(2, 1, q, 8, half=1)
-        share(2, 1, q, 7)
+        share(1, 1, q)
+        if q == 2:
+            wide_arrive(2, 1, q, 7)
+        else:
+            wide_arrive(2, 1, q, 7, half=0)
+            wide_arrive(2, 1, q, 8, half=1)
+        share(2, 1, q)
 
     def shared(q):
-        order = ((0, 0), (3, 0), (1, 0), (2, 0), (0, 1), (3, 1), (1, 1), (2, 1))
-        for sem, (dx, flip) in enumerate(order + ((0, 0),) * (q == 0)):
-            half = {0: 1, 8: 0}.get(sem) if q == 0 else None
-            ref = wide_ref.at[wide_id(dx, flip, 1), :, quarter_lanes(q, half)]
-            described(ref, sib_send.at[sem, q], sib_recv.at[sem, q], sib).wait_recv()
+        ref = wide_ref.at[pl.ds(0, WIDE // 2), :, quarter_lanes(q)]
+        described(ref, sib_send, sib_recv.at[q], sib).wait_recv()
 
     def multiply(q, part):
         start = quarter_start(z, yl, q)
@@ -237,24 +278,30 @@
 
     a2a(NEAR)
     a2a(FAR)
+    first_half()
     a2a(OPPOSITE)
     a2a(1)
-    first_half()
     near_send_group(0, NEAR, (4, 5, 7), 0)
     near_send_group(0, FAR, (4, 5, 6, 7), 2)
+    ready(0)
     own(0)
+    to_partner(0)
+    partner_first()
     a2a(NEAR + 1)
     a2a(FAR + 1)
     a2a(OPPOSITE + 1)
     near_send_group(0, NEAR, (1, 2, 3, 6), 1)
     near_send_group(0, FAR, (1, 2, 3), 3)
+    ready(1)
     own(1)
     to_partner(1)
     neighbours(0)
     partner(0)
-    near_send_group(0, 1, (4, 5, 6, 7), 4)
-    near_send_group(0, 1, (1, 2, 3), 13)
+    near_send_group(0, 1, (2, 5, 6, 7), 4)
     neighbours(1)
+    ready(2)
+    to_partner(2)
+    near_send_group(0, 1, (1, 3, 4), 13)
     opposite(0)
     partner_neighbours(0)
     own(2)
@@ -263,11 +310,6 @@
     near_arrive(3, NEAR, 0)
     near_send_group(NEAR, FAR, (4 ^ FAR, 5 ^ FAR, 7 ^ FAR), 6)
     partner(1)
-    near_arrive(4, 1, 4)
-    near_send_group(1, NEAR, (4, 5, 7), 7)
-    near_send_group(1, FAR, (1, 2, 3), 10)
-    near_send_group(1, NEAR, (2, 6), 8)
-    to_partner(2)
     partner_opposite(0)
     near_arrive(4, NEAR, 1)
     shared(0)
@@ -276,19 +318,19 @@
     local[2].wait()
     multiply(0, 0)
     multiply(0, 1)
+    near_arrive(4, 1, 4)
+    near_send_group(1, NEAR, (7, 4), 7)
+    near_send_group(1, FAR, (4, 6), 9)
+    near_send_group(1, NEAR, (5, 2), 8)
+    near_send_group(1, FAR, (3, 1), 10)
     multiply(0, 2)
     neighbours(2)
     multiply(0, 3)
     partner_neighbours(1)
+    ready(3)
     own(3)
     to_partner(3)
-    near_arrive(3, 1, 13)
-    near_send_group(1, NEAR, (1,), 7)
-    near_send_group(1, FAR, (4, 6, 7), 9)
-    near_send_group(1, NEAR, (3,), 8)
-    near_send_group(1, FAR, (5,), 10)
     opposite(1)
-    partner(2)
     partner_opposite(1)
     near_arrive(3, FAR, 3)
     near_arrive(4, OPPOSITE, 5)
@@ -296,38 +338,42 @@
     shared(1)
     local[3].wait()
     multiply(1, 0)
+    near_arrive(3, 1, 13)
+    near_send_group(1, NEAR, (3, 1, 6), 8)
+    near_send_group(1, FAR, (7, 5, 2), 10)
+    partner(2)
+    opposite(2)
+    opposite_to_partner(2)
     multiply(1, 1)
     multiply(1, 2)
+    partner(3)
     neighbours(3)
     multiply(1, 3)
+    near_arrive(2, FAR + 1, 9)
+    near_send_group(FAR + 1, NEAR, (4 ^ NEAR, 6 ^ NEAR), 11)
+    near_arrive(2, NEAR + 1, 7)
+    near_send_group(NEAR + 1, FAR, (4 ^ FAR, 7 ^ FAR), 12)
+    near_send_group(OPPOSITE, 1, (3, 5, 7), 14)
     partner_neighbours(2)
-    partner(3)
-    near_arrive(3, FAR + 1, 9)
-    near_send_group(FAR + 1, NEAR, (4 ^ NEAR, 6 ^ NEAR, 7 ^ NEAR), 11)
-    near_arrive(4, NEAR + 1, 7)
-    near_send_group(NEAR + 1, FAR, (1 ^ FAR, 4 ^ FAR, 5 ^ FAR, 7 ^ FAR), 12)
-    opposite(2)
-    opposite(3)
+    partner_neighbours(3)
     partner_opposite(2)
-    near_arrive(3, NEAR + 1, 8)
+    near_arrive(5, NEAR + 1, 8)
     shared(2)
     local[4].wait()
     multiply(2, 0)
-    partner_neighbours(3)
+    opposite(3)
     multiply(2, 1)
     multiply(2, 2)
+    partner_opposite(3)
     multiply(2, 3)
-    partner_opposite(3)
-    near_arrive(4, FAR + 1, 10)
-    near_arrive(3, OPPOSITE + 1, 11)
-    near_arrive(4, OPPOSITE + 1, 12)
+    near_arrive(5, FAR + 1, 10)
+    near_arrive(2, OPPOSITE + 1, 11)
+    near_arrive(2, OPPOSITE + 1, 12)
+    near_arrive(3, OPPOSITE + 1, 14)
     shared(3)
     local[5].wait()
-    for copy in sent:
-        copy.wait_send()
-    for sem, (count, source, receiver) in groups.items():
-        ref = narrow_ref.at[pl.ds(0, count), :, slice_lanes(source)]
-        described(ref, near_send.at[sem], near_recv.at[sem], at_narrow(receiver)).wait_send()
+    for panels, sem in ((7, far_send), (8, sib_send), (7, near_send)):
+        described(wide_ref.at[pl.ds(0, panels)], sem, sem, sib).wait_send()
 
 
 def finish_kernel(wide_ref, narrow_ref, sum_ref, out_ref, stage, sems):
@@ -362,8 +408,7 @@
         in_specs=[vmem],
         out_specs=(vmem, vmem, vmem),
         scratch_shapes=[
-            dma((7,)), dma((7,)), dma((6,)),
-            dma((14, 4)), dma((14, 4)), dma((9, 4)), dma((9, 4)), dma((14,)), dma((14,)),
+            dma((7,)), dma((6,)), dma(()), dma((14, 4)), dma(()), dma((4,)), dma(()), dma((15,)),
         ],
         compiler_params=pltpu.CompilerParams(collective_id=0, has_side_effects=True, vmem_limit_bytes=10 * 1024 * 1024),
     )(own)
@@ -378,8 +423,7 @@
 
 
 def shards(dosages, allele_counts, called_counts):
-    standard = standardize(dosages, allele_counts, called_counts)
-    own = standard.T.reshape(NARROW, SUB, PIECE)
+    own = standardize(dosages, allele_counts, called_counts)
     return product(own).reshape(WIDE, 1, SUB, BLK)
 
 

time: 82.6 us -> 76.5 us (0.926)
  other arithmetic: 3.03 us -> 0 us
  Pallas kernels: 79 us -> 76.2 us
    pallas_call x1, Pallas kernels: 70.9 us -> 66.3 us  [product(): pl.pallas_call(gather_kernel, out_shape=(pltpu.VMEM((WIDE, SUB, SNPS), jn...]
    transpose x1 -> x0, other arithmetic: 2.32 us -> none  [shards(): own = standard.T.reshape(NARROW, SUB, PIECE)]
    pallas_call x0 -> x1, Pallas kernels: none -> 1.77 us  [standardize(): pl.pallas_call(standardize_kernel, out_shape=pltpu.VMEM((NARROW, SUB, PIE...]
where the time goes in v4:
time: 76.5 us; the launch traced here: 76.4 us
  Pallas kernels  76.2 us (100%)
    pallas_call x1, Pallas kernels, product(): pl.pallas_call(gather_kernel, out_shape=(pltpu.VMEM((WIDE, SUB, SNPS), jn...  66.3 us
    pallas_call x1, Pallas kernels, product(): pl.pallas_call(finish_kernel, out_shape=jax.ShapeDtypeStruct((WIDE * SUB,...  8.11 us
    pallas_call x1, Pallas kernels, standardize(): pl.pallas_call(standardize_kernel, out_shape=pltpu.VMEM((NARROW, SUB, PIE...  1.77 us

profile of v4, /device:TPU:1, one launch (start us, length us, event | category | flops | bytes accessed | tf_op | source)
XLA Modules:
  0.0 76.4 jit_solution(16241238300350691439)
XLA Ops:
  0.0 1.8 %shard_map.37.own_ref = bf16[8,192,256]{2,1,0:T(8,128)(2,1)S(1)} custom-call(s32[256,1536]{1,0:T(8,128)} %dosages_ref.1, s32[1,256]{1,0:T(1,128)} %bitcast.5, s32[1,256]{1,0:T(1,128)} %bitcast.6), custom_call_target="tpu_custom_call" | custom-call | tf_op jit(solution)/shard_map/pallas_call | solution.py:51
  1.8 66.3 %shard_map.38 = (bf16[16,192,2048]{2,1,0:T(8,128)(2,1)S(1)}, bf16[8,192,2048]{2,1,0:T(8,128)(2,1)S(1)}, f32[3072,1536]{1,0:T(8,128)S(1)}) custom-call(bf16[8,192,256]{2,1,0:T(8,128)(2,1)S(1)} %shard_map.37.own_ref), custom_call_target="tpu_custom_call" | custom-call | tf_op jit(solution)/shard_map/pallas_call | solution.py:401
  68.1 8.1 %shard_map.39 = f32[3072,1536]{1,0:T(8,128)} custom-call(bf16[16,192,2048]{2,1,0:T(8,128)(2,1)S(1)} %get-tuple-element.8.wide_ref, bf16[8,192,2048]{2,1,0:T(8,128)(2,1)S(1)} %get-tuple-element.9.narrow_ref, f32[3072,1536]{1,0:T(8,128)S(1)} %get-tuple-element.10.sum_ref), custom_call_target="tpu_custom_call" | custom-call | tf_op jit(solution)/shard_map/pallas_call | solution.py:415

commit v5 on v4

--- a/solution.py
+++ b/solution.py
@@ -17,6 +17,7 @@
 SLOTS = 4
 ROWS = WIDE // PARTS * SUB
 NEAR, OPPOSITE, FAR = 2, 4, 6
+ARRIVAL = {NEAR: 0, FAR: 1, OPPOSITE: 1, 1: 2, NEAR + 1: 2, FAR + 1: 3, OPPOSITE + 1: 3}
 
 
 def standardize_kernel(dosages_ref, allele_hbm, called_hbm, out_ref, blocks, allele_ref, called_ref, sems):
@@ -126,15 +127,15 @@
             src_ref=src, dst_ref=dst, send_sem=ssem, recv_sem=rsem, device_id=device, device_id_type=MESH
         ).start()
 
-    def described(ref, ssem, rsem, device):
+    def described(ref, ssem, rsem):
         return pltpu.make_async_remote_copy(
-            src_ref=ref, dst_ref=ref, send_sem=ssem, recv_sem=rsem, device_id=device, device_id_type=MESH
+            src_ref=ref, dst_ref=ref, send_sem=ssem, recv_sem=rsem, device_id=sib, device_id_type=MESH
         )
 
     def a2a(label):
         send(
             own_ref.at[narrow_id(label)], wide_ref.at[w, :, slice_lanes(0)],
-            near_send, a2a_recv.at[label - 1], at_narrow(label),
+            near_send, a2a_recv.at[ARRIVAL[label]], at_narrow(label),
         )
 
     own_piece = pltpu.make_async_copy(own_ref.at[n], wide_ref.at[w, :, slice_lanes(0)], local_sem.at[4])
@@ -157,16 +158,19 @@
             send(src, narrow_ref.at[k, :, lanes], near_send, near_recv.at[sem], at_narrow(receiver))
 
     def near_arrive(count, source, sem):
-        ref = narrow_ref.at[pl.ds(0, count), :, slice_lanes(source)]
-        described(ref, near_send, near_recv.at[sem], at_narrow(1)).wait_recv()
+        ref = wide_ref.at[pl.ds(0, count), :, slice_lanes(source)]
+        described(ref, near_send, near_recv.at[sem]).wait_recv()
+
+    def far(sem, q):
+        return 32 + sem - 9 if 9 <= sem <= 11 else {6: 5, 7: 6, 8: 6, 12: 7, 13: 7}.get(sem, sem) * 4 + q
 
     def wide_send(dx, flip, q, sem, device, half=None):
         ref = wide_ref.at[wide_id(dx, flip, 0), :, quarter_lanes(q, half)]
-        send(ref, ref, far_send, far_recv.at[sem, q], device)
+        send(ref, ref, far_send, far_recv.at[far(sem, q)], device)
 
     def wide_arrive(dx, flip, q, sem, half=None):
         ref = wide_ref.at[wide_id(dx, flip, 0), :, quarter_lanes(q, half)]
-        described(ref, far_send, far_recv.at[sem, q], yhp).wait_recv()
+        described(ref, far_send, far_recv.at[far(sem, q)]).wait_recv()
 
     def share(dx, flip, q, half=None):
         ref = wide_ref.at[wide_id(dx, flip, 0), :, quarter_lanes(q, half)]
@@ -175,15 +179,13 @@
     def first_half():
         src, dst = own_ref.at[n], wide_ref.at[w, :, quarter_lanes(0, 0)]
         for sem, device in ((9, xp), (10, xm), (11, yhp)):
-            send(src, dst, far_send, far_recv.at[sem, 0], device)
+            send(src, dst, far_send, far_recv.at[far(sem, 0)], device)
         send(src, dst, sib_send, sib_recv.at[0], sib)
 
     def ready(q):
-        labels = ((NEAR,), (FAR, OPPOSITE), (1, NEAR + 1), (FAR + 1, OPPOSITE + 1))[q]
-        for label in labels:
-            ref = wide_ref.at[w, :, slice_lanes(label)]
-            described(ref, near_send, a2a_recv.at[label - 1], at_narrow(1)).wait_recv()
         lanes = quarter_lanes(q, None if q else 1)
+        ref = wide_ref.at[w, :, lanes]
+        described(ref, near_send, a2a_recv.at[q]).wait_recv()
         copy = pltpu.make_async_copy(wide_ref.at[w, :, lanes], narrow_ref.at[n, :, lanes], local_sem.at[q])
         copy.start()
         local.append(copy)
@@ -214,8 +216,7 @@
         share(1, 0, q)
 
     def opposite(q):
-        wide_arrive(2, 0, q, 5, half=0)
-        wide_arrive(2, 0, q, 6, half=1)
+        wide_arrive(2, 0, q, 5)
         share(2, 0, q)
 
     def opposite_to_partner(q):
@@ -247,20 +248,15 @@
         wide_send(1, 1, q, 8, xm, half=1)
 
     def partner_opposite(q):
-        wide_arrive(3, 1, q, 12, half=1)
+        wide_arrive(3, 1, q, 12)
         share(3, 1, q)
-        wide_arrive(1, 1, q, 13, half=0)
         share(1, 1, q)
-        if q == 2:
-            wide_arrive(2, 1, q, 7)
-        else:
-            wide_arrive(2, 1, q, 7, half=0)
-            wide_arrive(2, 1, q, 8, half=1)
+        wide_arrive(2, 1, q, 7)
         share(2, 1, q)
 
     def shared(q):
         ref = wide_ref.at[pl.ds(0, WIDE // 2), :, quarter_lanes(q)]
-        described(ref, sib_send, sib_recv.at[q], sib).wait_recv()
+        described(ref, sib_send, sib_recv.at[q]).wait_recv()
 
     def multiply(q, part):
         start = quarter_start(z, yl, q)
@@ -281,8 +277,8 @@
     first_half()
     a2a(OPPOSITE)
     a2a(1)
-    near_send_group(0, NEAR, (4, 5, 7), 0)
-    near_send_group(0, FAR, (4, 5, 6, 7), 2)
+    near_send_group(0, NEAR, (1, 4, 5, 7), 0)
+    near_send_group(0, FAR, (4, 6, 7), 2)
     ready(0)
     own(0)
     to_partner(0)
@@ -290,28 +286,28 @@
     a2a(NEAR + 1)
     a2a(FAR + 1)
     a2a(OPPOSITE + 1)
-    near_send_group(0, NEAR, (1, 2, 3, 6), 1)
-    near_send_group(0, FAR, (1, 2, 3), 3)
     ready(1)
     own(1)
     to_partner(1)
+    near_send_group(0, NEAR, (2, 3, 6), 1)
+    near_send_group(0, FAR, (1, 2, 3, 5), 3)
     neighbours(0)
     partner(0)
     near_send_group(0, 1, (2, 5, 6, 7), 4)
     neighbours(1)
     ready(2)
     to_partner(2)
-    near_send_group(0, 1, (1, 3, 4), 13)
+    near_send_group(0, 1, (1, 3, 4), 5)
     opposite(0)
     partner_neighbours(0)
     own(2)
-    near_arrive(4, FAR, 2)
-    near_send_group(FAR, NEAR, (4 ^ NEAR, 5 ^ NEAR, 6 ^ NEAR, 7 ^ NEAR), 5)
-    near_arrive(3, NEAR, 0)
-    near_send_group(NEAR, FAR, (4 ^ FAR, 5 ^ FAR, 7 ^ FAR), 6)
+    near_arrive(3, FAR, 2)
+    near_send_group(FAR, NEAR, (4 ^ NEAR, 6 ^ NEAR, 7 ^ NEAR), 3)
+    near_arrive(4, NEAR, 0)
+    near_send_group(NEAR, FAR, (1 ^ FAR, 4 ^ FAR, 5 ^ FAR, 7 ^ FAR), 3)
     partner(1)
     partner_opposite(0)
-    near_arrive(4, NEAR, 1)
+    near_arrive(3, NEAR, 1)
     shared(0)
     local[0].wait()
     local[1].wait()
@@ -319,10 +315,10 @@
     multiply(0, 0)
     multiply(0, 1)
     near_arrive(4, 1, 4)
-    near_send_group(1, NEAR, (7, 4), 7)
-    near_send_group(1, FAR, (4, 6), 9)
-    near_send_group(1, NEAR, (5, 2), 8)
-    near_send_group(1, FAR, (3, 1), 10)
+    near_send_group(1, NEAR, (7, 4), 6)
+    near_send_group(1, FAR, (4, 6), 8)
+    near_send_group(1, NEAR, (5, 2), 7)
+    near_send_group(1, FAR, (3, 1), 9)
     multiply(0, 2)
     neighbours(2)
     multiply(0, 3)
@@ -332,15 +328,13 @@
     to_partner(3)
     opposite(1)
     partner_opposite(1)
-    near_arrive(3, FAR, 3)
-    near_arrive(4, OPPOSITE, 5)
-    near_arrive(3, OPPOSITE, 6)
+    near_arrive(11, FAR, 3)
     shared(1)
     local[3].wait()
     multiply(1, 0)
-    near_arrive(3, 1, 13)
-    near_send_group(1, NEAR, (3, 1, 6), 8)
-    near_send_group(1, FAR, (7, 5, 2), 10)
+    near_arrive(3, 1, 5)
+    near_send_group(1, NEAR, (3, 1, 6), 7)
+    near_send_group(1, FAR, (7, 5, 2), 9)
     partner(2)
     opposite(2)
     opposite_to_partner(2)
@@ -349,31 +343,28 @@
     partner(3)
     neighbours(3)
     multiply(1, 3)
-    near_arrive(2, FAR + 1, 9)
-    near_send_group(FAR + 1, NEAR, (4 ^ NEAR, 6 ^ NEAR), 11)
-    near_arrive(2, NEAR + 1, 7)
-    near_send_group(NEAR + 1, FAR, (4 ^ FAR, 7 ^ FAR), 12)
-    near_send_group(OPPOSITE, 1, (3, 5, 7), 14)
+    near_arrive(2, FAR + 1, 8)
+    near_send_group(FAR + 1, NEAR, (4 ^ NEAR, 6 ^ NEAR), 9)
+    near_arrive(2, NEAR + 1, 6)
+    near_send_group(NEAR + 1, FAR, (4 ^ FAR, 7 ^ FAR), 9)
+    near_send_group(OPPOSITE, 1, (3, 5, 7), 9)
     partner_neighbours(2)
-    partner_neighbours(3)
     partner_opposite(2)
-    near_arrive(5, NEAR + 1, 8)
+    near_arrive(5, NEAR + 1, 7)
     shared(2)
     local[4].wait()
     multiply(2, 0)
-    opposite(3)
+    partner_neighbours(3)
     multiply(2, 1)
     multiply(2, 2)
+    opposite(3)
     partner_opposite(3)
     multiply(2, 3)
-    near_arrive(5, FAR + 1, 10)
-    near_arrive(2, OPPOSITE + 1, 11)
-    near_arrive(2, OPPOSITE + 1, 12)
-    near_arrive(3, OPPOSITE + 1, 14)
+    near_arrive(12, FAR + 1, 9)
     shared(3)
     local[5].wait()
     for panels, sem in ((7, far_send), (8, sib_send), (7, near_send)):
-        described(wide_ref.at[pl.ds(0, panels)], sem, sem, sib).wait_send()
+        described(wide_ref.at[pl.ds(0, panels)], sem, sem).wait_send()
 
 
 def finish_kernel(wide_ref, narrow_ref, sum_ref, out_ref, stage, sems):
@@ -381,7 +372,7 @@
     start = quarter_start(n // 2, n % 2, 3)
     copies = []
     panel = 0
-    for i, count in enumerate((1, 1, 2, 2, 2, 2, 2, 2, 2)):
+    for i, count in enumerate((2,) * (WIDE // 2)):
         slot, rows = i % SLOTS, slice(panel * SUB, (panel + count) * SUB)
         if i >= SLOTS:
             copies[i - SLOTS].wait()
@@ -408,7 +399,7 @@
         in_specs=[vmem],
         out_specs=(vmem, vmem, vmem),
         scratch_shapes=[
-            dma((7,)), dma((6,)), dma(()), dma((14, 4)), dma(()), dma((4,)), dma(()), dma((15,)),
+            dma((4,)), dma((6,)), dma(()), dma((35,)), dma(()), dma((4,)), dma(()), dma((10,)),
         ],
         compiler_params=pltpu.CompilerParams(collective_id=0, has_side_effects=True, vmem_limit_bytes=10 * 1024 * 1024),
     )(own)

time: 76.5 us -> 73.9 us (0.966)
  Pallas kernels: 76.2 us -> 73.6 us
    pallas_call x1, Pallas kernels: 66.3 us -> 64.3 us  [product(): pl.pallas_call(gather_kernel, out_shape=(pltpu.VMEM((WIDE, SUB, SNPS), jn...]
where the time goes in v5:
time: 73.9 us; the launch traced here: 73.8 us
  Pallas kernels  73.6 us (100%)
    pallas_call x1, Pallas kernels, product(): pl.pallas_call(gather_kernel, out_shape=(pltpu.VMEM((WIDE, SUB, SNPS), jn...  64.3 us
    pallas_call x1, Pallas kernels, product(): pl.pallas_call(finish_kernel, out_shape=jax.ShapeDtypeStruct((WIDE * SUB,...  7.51 us
    pallas_call x1, Pallas kernels, standardize(): pl.pallas_call(standardize_kernel, out_shape=pltpu.VMEM((NARROW, SUB, PIE...  1.77 us

profile of v5, /device:TPU:1, one launch (start us, length us, event | category | flops | bytes accessed | tf_op | source)
XLA Modules:
  0.0 73.8 jit_solution(17233183915035758290)
XLA Ops:
  0.0 1.8 %shard_map.37.own_ref = bf16[8,192,256]{2,1,0:T(8,128)(2,1)S(1)} custom-call(s32[256,1536]{1,0:T(8,128)} %dosages_ref.1, s32[1,256]{1,0:T(1,128)} %bitcast.5, s32[1,256]{1,0:T(1,128)} %bitcast.6), custom_call_target="tpu_custom_call" | custom-call | tf_op jit(solution)/shard_map/pallas_call | solution.py:52
  1.8 64.3 %shard_map.38 = (bf16[16,192,2048]{2,1,0:T(8,128)(2,1)S(1)}, bf16[8,192,2048]{2,1,0:T(8,128)(2,1)S(1)}, f32[3072,1536]{1,0:T(8,128)S(1)}) custom-call(bf16[8,192,256]{2,1,0:T(8,128)(2,1)S(1)} %shard_map.37.own_ref), custom_call_target="tpu_custom_call" | custom-call | tf_op jit(solution)/shard_map/pallas_call | solution.py:392
  66.1 7.5 %shard_map.39 = f32[3072,1536]{1,0:T(8,128)} custom-call(bf16[16,192,2048]{2,1,0:T(8,128)(2,1)S(1)} %get-tuple-element.8.wide_ref, bf16[8,192,2048]{2,1,0:T(8,128)(2,1)S(1)} %get-tuple-element.9.narrow_ref, f32[3072,1536]{1,0:T(8,128)S(1)} %get-tuple-element.10.sum_ref), custom_call_target="tpu_custom_call" | custom-call | tf_op jit(solution)/shard_map/pallas_call | solution.py:406

commit v6 on v5

--- a/solution.py
+++ b/solution.py
@@ -313,35 +313,35 @@
     local[1].wait()
     local[2].wait()
     multiply(0, 0)
+    neighbours(2)
     multiply(0, 1)
     near_arrive(4, 1, 4)
     near_send_group(1, NEAR, (7, 4), 6)
     near_send_group(1, FAR, (4, 6), 8)
     near_send_group(1, NEAR, (5, 2), 7)
     near_send_group(1, FAR, (3, 1), 9)
-    multiply(0, 2)
-    neighbours(2)
-    multiply(0, 3)
     partner_neighbours(1)
     ready(3)
     own(3)
     to_partner(3)
+    multiply(0, 2)
+    multiply(0, 3)
     opposite(1)
+    partner(2)
+    opposite(2)
     partner_opposite(1)
+    near_arrive(3, 1, 5)
+    near_send_group(1, NEAR, (3, 1, 6), 7)
+    near_send_group(1, FAR, (7, 5, 2), 9)
     near_arrive(11, FAR, 3)
     shared(1)
     local[3].wait()
     multiply(1, 0)
-    near_arrive(3, 1, 5)
-    near_send_group(1, NEAR, (3, 1, 6), 7)
-    near_send_group(1, FAR, (7, 5, 2), 9)
-    partner(2)
-    opposite(2)
+    partner(3)
     opposite_to_partner(2)
     multiply(1, 1)
+    neighbours(3)
     multiply(1, 2)
-    partner(3)
-    neighbours(3)
     multiply(1, 3)
     near_arrive(2, FAR + 1, 8)
     near_send_group(FAR + 1, NEAR, (4 ^ NEAR, 6 ^ NEAR), 9)

time: 73.9 us -> 73.6 us (level)
  no operation moved by 1% of the time
where the time goes in v6:
time: 73.6 us; the launch traced here: 73.5 us
  Pallas kernels  73.3 us (100%)
    pallas_call x1, Pallas kernels, product(): pl.pallas_call(gather_kernel, out_shape=(pltpu.VMEM((WIDE, SUB, SNPS), jn...  64 us
    pallas_call x1, Pallas kernels, product(): pl.pallas_call(finish_kernel, out_shape=jax.ShapeDtypeStruct((WIDE * SUB,...  7.51 us
    pallas_call x1, Pallas kernels, standardize(): pl.pallas_call(standardize_kernel, out_shape=pltpu.VMEM((NARROW, SUB, PIE...  1.77 us

profile of v6, /device:TPU:1, one launch (start us, length us, event | category | flops | bytes accessed | tf_op | source)
XLA Modules:
  0.0 73.5 jit_solution(8813584968275200513)
XLA Ops:
  0.0 1.8 %shard_map.37.own_ref = bf16[8,192,256]{2,1,0:T(8,128)(2,1)S(1)} custom-call(s32[256,1536]{1,0:T(8,128)} %dosages_ref.1, s32[1,256]{1,0:T(1,128)} %bitcast.5, s32[1,256]{1,0:T(1,128)} %bitcast.6), custom_call_target="tpu_custom_call" | custom-call | tf_op jit(solution)/shard_map/pallas_call | solution.py:52
  1.8 64.0 %shard_map.38 = (bf16[16,192,2048]{2,1,0:T(8,128)(2,1)S(1)}, bf16[8,192,2048]{2,1,0:T(8,128)(2,1)S(1)}, f32[3072,1536]{1,0:T(8,128)S(1)}) custom-call(bf16[8,192,256]{2,1,0:T(8,128)(2,1)S(1)} %shard_map.37.own_ref), custom_call_target="tpu_custom_call" | custom-call | tf_op jit(solution)/shard_map/pallas_call | solution.py:392
  65.8 7.5 %shard_map.39 = f32[3072,1536]{1,0:T(8,128)} custom-call(bf16[16,192,2048]{2,1,0:T(8,128)(2,1)S(1)} %get-tuple-element.8.wide_ref, bf16[8,192,2048]{2,1,0:T(8,128)(2,1)S(1)} %get-tuple-element.9.narrow_ref, f32[3072,1536]{1,0:T(8,128)S(1)} %get-tuple-element.10.sum_ref), custom_call_target="tpu_custom_call" | custom-call | tf_op jit(solution)/shard_map/pallas_call | solution.py:406
